TPU v7x, 128 devices: a whole 4x4x4 slice. The times are simulated.
128 devices in a mesh: space: 16 (over z_hi, x, core), band: 8 (over z_lo, y).
Axes of the slice: x: 4, y: 4, z: 4 (z_hi: 2, z_lo: 2; z = z_hi * 2 + z_lo), core: 2. Of those that a mesh axis runs over, the one named last changes fastest.
Arguments:
- blocks: float32 [2, 32, 64, 6144], P(None, 'band', 'space'), may hold values from -304 to 304
- later: float32 [256, 64, 6144], P('band', 'space'), may hold values from -304 to 304
- potential: float32 [64, 6144], P('space'), may hold values from -1.5 to 1.5
Outputs:
- h_block: float32 [2, 32, 64, 6144], P(None, 'band', 'space')
- h_later: float32 [256, 64, 6144], P('band', 'space')
All inputs are finite; a program needn't handle non-finite values.
Results may differ from a plain program's by a relative error of at most 0.00009.
Values sent between devices are 32-bit elements; how exact they have to be, the bound alone decides.
A program may use at most 128 MiB of HBM per device.

v0:
```python
import jax
import jax.numpy as jnp
from jax import lax
from jax.sharding import PartitionSpec as P

NZ = 96
stencil_weights = (-205.0 / 72.0, 8.0 / 5.0, -1.0 / 5.0, 8.0 / 315.0, -1.0 / 560.0)


def extended_2(x, sides, width):
    for axis, dim in sides:
        size, length = (lax.axis_size(axis), x.shape[dim])
        up = [(i, (i + 1) % size) for i in range(size - 1)]
        down = [(j, i) for i, j in up]
        last = lax.slice_in_dim(x, length - width, length, axis=dim)
        initial = lax.slice_in_dim(x, 0, width, axis=dim)
        before = lax.ppermute(last, axis, up)
        after = lax.ppermute(initial, axis, down)
        x = jnp.concatenate([before, x, after], axis=dim)
    return x


def stencil(extended, potential, depth):
    center = extended[:, 4:-4]
    planes = center.shape[1]
    length = center.shape[2]
    laplace = 3.0 * stencil_weights[0] * center
    for step in range(1, 5):
        laplace = laplace + stencil_weights[step] * (
            extended[:, 4 + step : 4 + step + planes] + extended[:, 4 - step : 4 - step + planes]
        )
    margin = 4 * depth
    ypadded = jnp.pad(center, ((0, 0), (0, 0), (margin, margin)))
    for step in range(1, 5):
        upper = ypadded[:, :, margin + step * depth : margin + step * depth + length]
        lower = ypadded[:, :, margin - step * depth : margin - step * depth + length]
        laplace = laplace + stencil_weights[step] * (upper + lower)
    zpadded = jnp.pad(center, ((0, 0), (0, 0), (4, 4)))
    zpos = lax.broadcasted_iota(jnp.int32, (length,), 0) % depth
    for step in range(1, 5):
        upper = jnp.where(zpos + step < depth, zpadded[:, :, 4 + step : 4 + step + length], 0.0)
        lower = jnp.where(zpos - step >= 0, zpadded[:, :, 4 - step : 4 - step + length], 0.0)
        laplace = laplace + stencil_weights[step] * (upper + lower)
    return -0.5 * laplace + potential[None] * center


def inner(left, right):
    return jnp.dot(
        left, right.T, precision=lax.Precision.HIGHEST, preferred_element_type=jnp.float32
    )


def apply_rows(left, right):
    return jnp.dot(left, right, precision=lax.Precision.HIGHEST, preferred_element_type=jnp.float32)


def local(blocks, later, potential):
    own_rows = blocks.shape[1]
    planes = blocks.shape[2]
    length = blocks.shape[3]
    local_cells = planes * length
    cells = planes * lax.axis_size("space") * length
    later_count = later.shape[0]
    owned = 2 * own_rows
    offset = lax.axis_index("band") * own_rows
    later_flat = later.reshape(later_count, local_cells)
    gathered = lax.all_gather(blocks, "band", axis=1, tiled=True)
    block_rows = gathered.shape[1]
    flat = gathered.reshape(2, block_rows, local_cells)

    def orthonormal(rows):
        correlation = lax.psum(inner(rows, rows), "space") / cells
        lower = jnp.linalg.cholesky(correlation)
        return (lower, lax.linalg.triangular_solve(lower, rows, left_side=True, lower=True))

    lower_one, q_first = orthonormal(flat[0])
    crossed = lax.psum(inner(q_first, flat[1]), "space") / cells
    remainder = flat[1] - apply_rows(crossed.T, q_first)
    lower_two, q_second = orthonormal(remainder)
    weight_one = lax.psum(inner(q_first, later_flat), "space") / cells
    partial_later = later_flat - apply_rows(weight_one.T, q_first)
    weight_two = lax.psum(inner(q_second, partial_later), "space") / cells
    projected = partial_later - apply_rows(weight_two.T, q_second)
    mine_one = lax.dynamic_slice_in_dim(q_first, offset, own_rows, 0)
    mine_two = lax.dynamic_slice_in_dim(q_second, offset, own_rows, 0)
    states = jnp.concatenate([mine_one, mine_two, projected], axis=0).reshape(
        owned + later_count, planes, length
    )
    extended = extended_2(states, (("space", 1),), 4)
    applied = stencil(extended, potential, NZ)
    h_block = applied[:owned].reshape(blocks.shape)
    h_later = applied[owned:]
    return (h_block, h_later)


def solution(mesh):
    return jax.shard_map(
        local,
        mesh=mesh,
        in_specs=(P(None, "band", "space", None), P("band", "space", None), P("space", None)),
        out_specs=(P(None, "band", "space", None), P("band", "space", None)),
        check_vma=False,
    )
```

profile of v0, /device:TPU:64, one launch (start us, length us, event | category | flops | bytes accessed | tf_op | source)
XLA Modules:
  0.0 556.3 jit_solution(2565554386587875953)
XLA Ops:
  7.2 2.1 copy.17
  9.3 5.4 copy.37
  14.7 69.3 %all-gather.2.cloned.1.call-done = f32[2,32,4,6144]{3,2,0,1:T(4,128)} async-done(((f32[2,4,4,6144]{3,2,0,1:T(4,128)}), f32[2,32,4,6144]{3,2,0,1:T(4,128)}) %all-gather.2.cloned.1.call-update) | async-done | bytes 6291472 | tf_op jit(solution)/shard_map/all_gather | solution.py:67
  83.9 3.3 fusion.56
  87.2 3.5 copy.36
  90.7 4.2 fusion.35
  94.9 67.7 %psum.35 = f32[32,32]{0,1:T(8,128)S(1)} all-reduce(f32[32,32]{0,1:T(8,128)S(1)} %fusion.35), channel_id=1, replica_groups=mesh['space'=16,'band'=8] {'space'}, use_global_device_ids=true, to_apply=%region_0.0 | all-reduce | flops 1024 | bytes 8192 | tf_op jit(solution)/shard_map/psum | solution.py:72
  162.7 2.9 cholesky.44
  166.9 2.4 custom-call.6
  171.2 2.8 fusion.44
  174.1 2.7 fusion.57
  176.8 65.1 %psum.36 = f32[32,32]{0,1:T(8,128)S(1)} all-reduce(f32[32,32]{0,1:T(8,128)S(1)} %fusion.57), channel_id=1, replica_groups=mesh['space'=16,'band'=8] {'space'}, use_global_device_ids=true, to_apply=%region_3.6 | all-reduce | flops 1024 | bytes 8192 | tf_op jit(solution)/shard_map/psum | solution.py:77
  241.9 4.9 convolution_subtract_fusion.2
  248.4 2.6 fusion.58
  251.1 3.3 fusion.59
  254.4 66.3 %all-reduce.2 = (f32[32,32]{0,1:T(8,128)}, f32[32,32]{0,1:T(8,128)}) all-reduce(f32[32,32]{0,1:T(8,128)} %fusion.59, f32[32,32]{0,1:T(8,128)S(1)} %fusion.58), channel_id=1, replica_groups=mesh['space'=16,'band'=8] {'space'}, use_global_device_ids=true, to_apply=%region_5.8 | all-reduce | flops 2048 | bytes 16384 | tf_op jit(solution)/shard_map/psum | solution.py:80
  320.8 5.4 convolution_subtract_fusion.1
  326.3 2.9 cholesky.55
  330.5 2.4 custom-call.7
  333.0 4.8 fusion.41
  338.6 3.3 fusion.60
  341.9 65.8 %psum.39 = f32[32,32]{0,1:T(8,128)S(1)} all-reduce(f32[32,32]{0,1:T(8,128)} %fusion.60), channel_id=1, replica_groups=mesh['space'=16,'band'=8] {'space'}, use_global_device_ids=true, to_apply=%region_6.9 | all-reduce | flops 1024 | bytes 8192 | tf_op jit(solution)/shard_map/psum | solution.py:82
  407.7 4.7 convolution_subtract_fusion
  412.4 2.2 pad_maximum_fusion.2
  414.7 5.7 %reshape.36 = f32[40,4,6144]{2,1,0:T(4,128)} reshape(f32[40,24576]{1,0:T(8,128)} %pad_maximum_fusion.2) | data formatting | bytes 7864320 | tf_op jit(solution)/shard_map/reshape | solution.py:86
  420.3 1.9 collective-permute-start
  422.3 2.7 collective-permute-start.1
  425.1 40.7 %collective-permute-done = f32[40,4,6144]{2,1,0:T(4,128)} collective-permute-done((f32[40,4,6144]{2,1,0:T(4,128)}, f32[40,4,6144]{2,1,0:T(4,128)}, u32[]{:S(2)}, u32[]{:S(2)}) %collective-permute-start) | collective-permute-done | bytes 3932192 | tf_op jit(solution)/shard_map/ppermute | solution.py:18
  465.8 7.4 %collective-permute-done.1 = f32[40,4,6144]{2,1,0:T(4,128)} collective-permute-done((f32[40,4,6144]{2,1,0:T(4,128)}, f32[40,4,6144]{2,1,0:T(4,128)}, u32[]{:S(2)}, u32[]{:S(2)}) %collective-permute-start.1) | collective-permute-done | bytes 3932192 | tf_op jit(solution)/shard_map/ppermute | solution.py:17
  473.2 69.8 %multiply_add_fusion = f32[40,4,6144]{2,1,0:T(4,128)} fusion(f32[40,4,6144]{2,1,0:T(4,128)} %reshape.36, f32[40,4,6144]{2,1,0:T(4,128)} %collective-permute-done.1, f32[40,4,6144]{2,1,0:T(4,128)} %collective-permute-done, f32[4,6144]{1,0:T(4,128)S(1)} %copy-done.5, pred[6144]{0:T(1024)(128)(4,1)S(1)} %get-tuple-element.8, ...), kind=kLoop, calls=%fused_computation.33 | loop fusion | flops 53084160 | bytes 15876096 | tf_op jit(solution)/shard_map/add | solution.py:44
  543.0 2.1 slice.129
  545.1 3.9 slice.130
  (35 shorter events, 7.4 us)
Async XLA Ops:
  7.2 76.8 %all-gather.2.cloned.1.call-start = ((), (), s32[]{:S(2)}) async-start(), calls=%async_computation | async-start | bytes 7077888 | tf_op jit(solution)/shard_map/all_gather | solution.py:67
  171.2 2.8 copy-start.2
  246.8 1.7 copy-start
  248.4 2.7 copy-start.1
  320.8 5.4 copy-start.6
  333.0 5.7 %copy-start.3 = (f32[32,24576]{1,0:T(8,128)S(1)}, f32[32,24576]{1,0:T(8,128)}, u32[]{:S(2)}) copy-start(f32[32,24576]{1,0:T(8,128)} %convolution_subtract_fusion.1) | copy-start | bytes 9437188
  407.7 4.7 copy-start.4
  414.7 58.5 %copy-start.5 = (f32[4,6144]{1,0:T(4,128)S(1)}, f32[4,6144]{1,0:T(4,128)}, u32[]{:S(2)}) copy-start(f32[4,6144]{1,0:T(4,128)} %param.8) | copy-start | bytes 294916
  420.3 45.4 %collective-permute-start = (f32[40,4,6144]{2,1,0:T(4,128)}, f32[40,4,6144]{2,1,0:T(4,128)}, u32[]{:S(2)}, u32[]{:S(2)}) collective-permute-start(f32[40,4,6144]{2,1,0:T(4,128)} %reshape.36), channel_id=1, source_target_pairs={{8,0},{16,8},{24,16},{32,24},{40,32},{48,40},{56,48},{64,56},{72,6... | collective-permute-start | bytes 11796488 | tf_op jit(solution)/shard_map/ppermute | solution.py:18
  422.3 50.9 %collective-permute-start.1 = (f32[40,4,6144]{2,1,0:T(4,128)}, f32[40,4,6144]{2,1,0:T(4,128)}, u32[]{:S(2)}, u32[]{:S(2)}) collective-permute-start(f32[40,4,6144]{2,1,0:T(4,128)} %reshape.36), channel_id=1, source_target_pairs={{0,8},{8,16},{16,24},{24,32},{32,40},{40,48},{48,56},{56,64},{64,7... | collective-permute-start | bytes 11796488 | tf_op jit(solution)/shard_map/ppermute | solution.py:17
Sparse Core Ops, SparseCore 0:
  10.2 73.6 all-gather.1
where the time goes:
time: 563 us; the launch traced here: 556 us
  blocking collectives  265 us (47%)
  waiting for transfers between devices  117 us (21%)
  other arithmetic  85.5 us (15%)
  matrix products  38.7 us (7%)
  local copies, waits for them, and re-layouts  30.4 us (5%)
  between operations  14.7 us (3%)
    add x1, other arithmetic, stencil(): return -0.5 * laplace + potential[None] * center  69.8 us
    all_gather x1, waiting for transfers between devices, local(): gathered = lax.all_gather(blocks, 'band', axis=1, tiled=True)  69.3 us
    psum x1, blocking collectives, orthonormal(): correlation = lax.psum(inner(rows, rows), 'space') / cells  67.7 us
    psum x1, blocking collectives, local(): weight_one = lax.psum(inner(q_first, later_flat), 'space') / cells  66.3 us
    psum x1, blocking collectives, local(): weight_two = lax.psum(inner(q_second, partial_later), 'space') / cells  65.8 us
    psum x1, blocking collectives, local(): crossed = lax.psum(inner(q_first, flat[1]), 'space') / cells  65.1 us
    ppermute x1, waiting for transfers between devices, extended_2(): after = lax.ppermute(initial, axis, down)  40.7 us
    dot_general x5, matrix products, inner(): jnp.dot(left, right.T, precision=lax.Precision.HIGHEST, preferred_element...  16.1 us
  transfers between devices with their start and end apart: 3, of which 3 were waited for; matrix products, arithmetic and copies ran while one was open for 1% of the time, Pallas kernels for 0%

commit v1 on v0

--- a/solution.py
+++ b/solution.py
@@ -77,7 +77,7 @@
     crossed = lax.psum(inner(q_first, flat[1]), "space") / cells
     remainder = flat[1] - apply_rows(crossed.T, q_first)
     lower_two, q_second = orthonormal(remainder)
-    weight_one = lax.psum(inner(q_first, later_flat), "space") / cells
+    weight_one = jnp.sum(lax.all_gather(inner(q_first, later_flat), "space"), axis=0) / cells
     partial_later = later_flat - apply_rows(weight_one.T, q_first)
     weight_two = lax.psum(inner(q_second, partial_later), "space") / cells
     projected = partial_later - apply_rows(weight_two.T, q_second)

time: 563 us -> 589 us (1.046)
  blocking collectives: 265 us -> 286 us
    psum x1 -> x0, blocking collectives: 66.3 us -> none  [local(): weight_one = lax.psum(inner(q_first, later_flat), 'space') / cells]
    psum x1 -> x2, blocking collectives: 67.7 us -> 132 us  [orthonormal(): correlation = lax.psum(inner(rows, rows), 'space') / cells]
    all_gather x0 -> x1, blocking collectives: none -> 21.5 us  [local(): lax.all_gather(inner(q_first, later_flat), 'space')]
    unnamed x18 -> x22, local copies, waits for them, and re-layouts: 14.5 us -> 17.7 us
where the time goes in v1:
time: 589 us; the launch traced here: 582 us
  blocking collectives  286 us (49%)
  waiting for transfers between devices  118 us (20%)
  other arithmetic  87.1 us (15%)
  matrix products  37.7 us (6%)
  local copies, waits for them, and re-layouts  34.4 us (6%)
  between operations  14.4 us (2%)
    psum x2, blocking collectives, orthonormal(): correlation = lax.psum(inner(rows, rows), 'space') / cells  132 us
    add x1, other arithmetic, stencil(): return -0.5 * laplace + potential[None] * center  69.8 us
    all_gather x1, waiting for transfers between devices, local(): gathered = lax.all_gather(blocks, 'band', axis=1, tiled=True)  69.3 us
    psum x1, blocking collectives, local(): weight_two = lax.psum(inner(q_second, partial_later), 'space') / cells  67.4 us
    psum x1, blocking collectives, local(): crossed = lax.psum(inner(q_first, flat[1]), 'space') / cells  65.2 us
    ppermute x1, waiting for transfers between devices, extended_2(): after = lax.ppermute(initial, axis, down)  40.8 us
    all_gather x1, blocking collectives, local(): lax.all_gather(inner(q_first, later_flat), 'space')  21.5 us
    unnamed x22, local copies, waits for them, and re-layouts  17.7 us
  transfers between devices with their start and end apart: 3, of which 3 were waited for; matrix products, arithmetic and copies ran while one was open for 1% of the time, Pallas kernels for 0%

profile of v1, /device:TPU:64, one launch (start us, length us, event | category | flops | bytes accessed | tf_op | source)
XLA Modules:
  0.0 582.0 jit_solution(7154513997749898399)
XLA Ops:
  7.2 2.1 copy.17
  9.3 5.4 copy.36
  14.7 69.3 %all-gather.3.cloned.1.call-done = f32[2,32,4,6144]{3,2,0,1:T(4,128)} async-done(((f32[2,4,4,6144]{3,2,0,1:T(4,128)}), f32[2,32,4,6144]{3,2,0,1:T(4,128)}) %all-gather.3.cloned.1.call-update) | async-done | bytes 6291472 | tf_op jit(solution)/shard_map/all_gather | solution.py:67
  83.9 3.3 fusion.56
  87.2 3.5 copy.35
  90.7 4.2 fusion.35
  94.9 67.3 %psum.28 = f32[32,32]{0,1:T(8,128)S(1)} all-reduce(f32[32,32]{0,1:T(8,128)S(1)} %fusion.35), channel_id=1, replica_groups=mesh['space'=16,'band'=8] {'space'}, use_global_device_ids=true, to_apply=%region_0.0 | all-reduce | flops 1024 | bytes 8192 | tf_op jit(solution)/shard_map/psum | solution.py:72
  162.3 2.9 cholesky.44
  166.6 2.4 custom-call.6
  170.9 2.8 fusion.44
  173.7 2.7 fusion.57
  176.4 65.2 %psum.29 = f32[32,32]{0,1:T(8,128)S(1)} all-reduce(f32[32,32]{0,1:T(8,128)S(1)} %fusion.57), channel_id=1, replica_groups=mesh['space'=16,'band'=8] {'space'}, use_global_device_ids=true, to_apply=%region_3.6 | all-reduce | flops 1024 | bytes 8192 | tf_op jit(solution)/shard_map/psum | solution.py:77
  241.6 4.9 convolution_subtract_fusion.2
  248.1 2.6 fusion.58
  250.7 65.0 %psum.30 = f32[32,32]{0,1:T(8,128)S(1)} all-reduce(f32[32,32]{0,1:T(8,128)S(1)} %fusion.58), channel_id=1, replica_groups=mesh['space'=16,'band'=8] {'space'}, use_global_device_ids=true, to_apply=%region_4.7 | all-reduce | flops 1024 | bytes 8192 | tf_op jit(solution)/shard_map/psum | solution.py:72
  315.8 2.9 cholesky.55
  320.0 2.4 custom-call.7
  322.5 4.9 fusion.41
  329.9 2.7 fusion.59
  332.5 21.5 %all-gather = f32[512,32]{1,0:T(8,128)} all-gather(f32[32,32]{1,0:T(8,128)S(1)} %fusion.59), channel_id=2, replica_groups=mesh['space'=16,'band'=8] {'space'}, dimensions={0}, use_global_device_ids=true | all-gather | bytes 69632 | tf_op jit(solution)/shard_map/all_gather | solution.py:80
  356.4 5.0 convolution_subtract_fusion.1
  363.1 3.3 fusion.60
  366.3 67.4 %psum.31 = f32[32,32]{0,1:T(8,128)S(1)} all-reduce(f32[32,32]{0,1:T(8,128)} %fusion.60), channel_id=1, replica_groups=mesh['space'=16,'band'=8] {'space'}, use_global_device_ids=true, to_apply=%region_6.9 | all-reduce | flops 1024 | bytes 8192 | tf_op jit(solution)/shard_map/psum | solution.py:82
  433.7 4.7 convolution_subtract_fusion
  438.5 2.2 pad_maximum_fusion.2
  440.7 5.7 reshape.36
  448.3 2.6 collective-permute-start.1
  451.0 40.8 %collective-permute-done = f32[40,4,6144]{2,1,0:T(4,128)} collective-permute-done((f32[40,4,6144]{2,1,0:T(4,128)}, f32[40,4,6144]{2,1,0:T(4,128)}, u32[]{:S(2)}, u32[]{:S(2)}) %collective-permute-start) | collective-permute-done | bytes 3932192 | tf_op jit(solution)/shard_map/ppermute | solution.py:18
  491.8 7.4 %collective-permute-done.1 = f32[40,4,6144]{2,1,0:T(4,128)} collective-permute-done((f32[40,4,6144]{2,1,0:T(4,128)}, f32[40,4,6144]{2,1,0:T(4,128)}, u32[]{:S(2)}, u32[]{:S(2)}) %collective-permute-start.1) | collective-permute-done | bytes 3932192 | tf_op jit(solution)/shard_map/ppermute | solution.py:17
  499.2 69.8 %multiply_add_fusion = f32[40,4,6144]{2,1,0:T(4,128)} fusion(f32[40,4,6144]{2,1,0:T(4,128)} %reshape.36, f32[40,4,6144]{2,1,0:T(4,128)} %collective-permute-done.1, f32[40,4,6144]{2,1,0:T(4,128)} %collective-permute-done, f32[4,6144]{1,0:T(4,128)S(1)} %copy-done.8, pred[6144]{0:T(1024)(128)(4,1)S(1)} %get-tuple-element.6, ...), kind=kLoop, calls=%fused_computation.33 | loop fusion | flops 53084160 | bytes 15876096 | tf_op jit(solution)/shard_map/add | solution.py:44
  569.0 2.1 slice.129
  571.1 3.9 slice.130
  (42 shorter events, 14.9 us)
Async XLA Ops:
  7.2 76.8 %all-gather.3.cloned.1.call-start = ((), (), s32[]{:S(2)}) async-start(), calls=%async_computation | async-start | bytes 7077888 | tf_op jit(solution)/shard_map/all_gather | solution.py:67
  170.9 2.8 copy-start.5
  246.5 1.7 copy-start
  322.5 7.4 %copy-start.4 = (f32[4,8,4,6144]{3,1,2,0:T(8,128)S(1)}, f32[4,8,4,6144]{3,1,2,0:T(8,128)}, u32[]{:S(2)}) copy-start(f32[4,8,4,6144]{3,1,2,0:T(8,128)} %copy.36) | copy-start | bytes 9437188
  327.4 1.7 copy-start.1
  356.4 6.7 %copy-start.2 = (f32[32,24576]{1,0:T(8,128)S(1)}, f32[32,24576]{1,0:T(8,128)}, u32[]{:S(2)}) copy-start(f32[32,24576]{1,0:T(8,128)} %copy-done.1) | copy-start | bytes 9437188
  361.4 1.7 copy-start.6
  363.1 70.7 %copy-start.3 = (f32[32,24576]{1,0:T(8,128)S(1)}, f32[32,24576]{1,0:T(8,128)}, u32[]{:S(2)}) copy-start(f32[32,24576]{1,0:T(8,128)} %copy-done.1) | copy-start | bytes 9437188
  433.7 4.7 copy-start.7
  440.7 58.5 %copy-start.8 = (f32[4,6144]{1,0:T(4,128)S(1)}, f32[4,6144]{1,0:T(4,128)}, u32[]{:S(2)}) copy-start(f32[4,6144]{1,0:T(4,128)} %param.8) | copy-start | bytes 294916
  446.4 45.4 %collective-permute-start = (f32[40,4,6144]{2,1,0:T(4,128)}, f32[40,4,6144]{2,1,0:T(4,128)}, u32[]{:S(2)}, u32[]{:S(2)}) collective-permute-start(f32[40,4,6144]{2,1,0:T(4,128)} %reshape.36), channel_id=1, source_target_pairs={{8,0},{16,8},{24,16},{32,24},{40,32},{48,40},{56,48},{64,56},{72,6... | collective-permute-start | bytes 11796488 | tf_op jit(solution)/shard_map/ppermute | solution.py:18
  448.3 50.9 %collective-permute-start.1 = (f32[40,4,6144]{2,1,0:T(4,128)}, f32[40,4,6144]{2,1,0:T(4,128)}, u32[]{:S(2)}, u32[]{:S(2)}) collective-permute-start(f32[40,4,6144]{2,1,0:T(4,128)} %reshape.36), channel_id=1, source_target_pairs={{0,8},{8,16},{16,24},{24,32},{32,40},{40,48},{48,56},{56,64},{64,7... | collective-permute-start | bytes 11796488 | tf_op jit(solution)/shard_map/ppermute | solution.py:17
Sparse Core Ops, SparseCore 0:
  10.2 73.6 all-gather.2
